TPU v7x, 32 devices: a whole 2x2x4 slice. The times are simulated.
32 devices in a mesh: group: 2 (over x), frame: 4 (over y, core), strip: 4 (over z).
Axes of the slice: x: 2, y: 2, z: 4, core: 2. Of those that a mesh axis runs over, the one named last changes fastest.
Arguments:
- spatial_queries: bfloat16 [32, 1024, 576], P(('group', 'frame'), 'strip'), parts along dimension 0, may hold values from -6 to 6
- spatial_keys: bfloat16 [32, 1024, 576], P(('group', 'frame'), 'strip'), parts along dimension 0, may hold values from -6 to 6
- spatial_values: bfloat16 [32, 1024, 576], P(('group', 'frame'), 'strip'), parts along dimension 0, may hold values from -6 to 6
- hidden: bfloat16 [32, 1024, 1152], P(('group', 'frame'), 'strip'), parts along dimension 0, may hold values from -6 to 6
- spatial_out_weight: bfloat16 [576, 1152], replicated, may hold values from -0.25 to 0.25
- spatial_gain: float32 [1152], replicated, may hold values from 0.5 to 1.5
- temporal_qkv_weight: bfloat16 [1152, 1728], replicated, may hold values from -0.1875 to 0.1875
- temporal_out_weight: bfloat16 [576, 1152], replicated, may hold values from -0.25 to 0.25
- temporal_gain: float32 [1152], replicated, may hold values from 0.5 to 1.5
- tile_list: int32 [32, 8, 3], P(('group', 'frame'), 'strip'), parts along dimension 0, may hold values from 0 to 7, as said below
- tile_count: int32 [32, 8], P(('group', 'frame'), 'strip'), parts along dimension 0, may hold values from 1 to 3, as said below
Outputs:
- block_out: bfloat16 [32, 1024, 1152], P(('group', 'frame'), 'strip'), parts along dimension 0
There are 2 independent parts, one for each index of `group`. A program takes and returns all parts, laid end to end along the dimension named above; an argument that names none is the same for every part. Nothing has to cross between parts.
Inputs may be any that keep to these rules, and one draw needn't show every extreme that they name: `tile_list`: entry 0 of a query tile's row is the query tile itself; the 3 entries of a row are distinct tiles, each in the query tile's own strip of 2 tiles or the nearest tile of an adjacent strip of the same frame. In frame 0, the first tile of every strip but the first attends the tile just below it, and the last tile of every strip but the last attends the tile just above it. `tile_count`: some query tile has 3 in every draw.
All inputs are finite; a program needn't handle non-finite values.
Results may differ from a plain program's by a relative error of at most 0.0083.
Values may be sent and summed in bfloat16 or wider, within the bound.
No kernel may reach another device: no remote copies, remote signals or barrier semaphores. Data moves between devices by JAX's collectives and lax.ppermute only.
A program may use at most 128 MiB of HBM per device.

v0:
```python
import jax
import jax.numpy as jnp
from jax import lax
from jax.sharding import PartitionSpec as P

D = 1152
HEAD_DIM = 72
HEADS = 8
TILE = 128
TILES_DEV = 2
MAXT = 3


epsilon = 1e-06


def with_halo(x, sides, width):
    for axis, dim in sides:
        size, length = (lax.axis_size(axis), x.shape[dim])
        up = [(i, (i + 1) % size) for i in range(size - 1)]
        down = [(j, i) for i, j in up]
        last = lax.slice_in_dim(x, length - width, length, axis=dim)
        initial = lax.slice_in_dim(x, 0, width, axis=dim)
        before = lax.ppermute(last, axis, up)
        after = lax.ppermute(initial, axis, down)
        x = jnp.concatenate([before, x, after], axis=dim)
    return x


def head_norm(values):
    return values * lax.rsqrt(jnp.mean(values * values, axis=-1, keepdims=True) + epsilon)


def row_norm(values, gain):
    return values * lax.rsqrt(jnp.mean(values * values, axis=-1, keepdims=True) + epsilon) * gain


def spatial_attention(spatial_queries, spatial_keys, spatial_values, tile_list, tile_count):
    frames_here, tokens_here, width = spatial_queries.shape
    scale = HEAD_DIM ** (-0.5)
    span = TILES_DEV + 2
    normed_queries = head_norm(
        spatial_queries.astype(jnp.float32).reshape(frames_here, TILES_DEV, TILE, HEADS, HEAD_DIM)
    ).astype(jnp.bfloat16)
    normed_keys = head_norm(
        spatial_keys.astype(jnp.float32).reshape(frames_here, tokens_here, HEADS, HEAD_DIM)
    ).astype(jnp.bfloat16)
    key_value = jnp.concatenate(
        [normed_keys.reshape(frames_here, tokens_here, width), spatial_values], axis=2
    )
    padded = with_halo(key_value, (("strip", 1),), TILE)
    first_tile = lax.axis_index("strip") * TILES_DEV - 1
    local_list = tile_list - first_tile
    slot_live = jnp.arange(MAXT)[None, None, :] < tile_count[:, :, None]
    hits = (local_list[..., None] == jnp.arange(span)[None, None, None, :]) & slot_live[..., None]
    tile_mask = jnp.any(hits, axis=2).astype(jnp.float32)
    key_mask = jnp.repeat(tile_mask, TILE, axis=2)
    keys_all = padded[:, :, :width].reshape(frames_here, span * TILE, HEADS, HEAD_DIM)
    values_all = padded[:, :, width:].reshape(frames_here, span * TILE, HEADS, HEAD_DIM)
    scores = (
        jnp.einsum(
            "ftqhd,fkhd->fthqk", normed_queries, keys_all, preferred_element_type=jnp.float32
        )
        * scale
    )
    expo = jnp.exp(scores) * key_mask[:, :, None, None, :]
    total = jnp.sum(expo, axis=4)
    numer = jnp.einsum(
        "fthqk,fkhd->ftqhd",
        expo.astype(jnp.bfloat16),
        values_all,
        preferred_element_type=jnp.float32,
    )
    result = numer / jnp.transpose(total, (0, 1, 3, 2))[..., None]
    return result.astype(jnp.bfloat16).reshape(frames_here, tokens_here, width)


def split_heads(qkv_rows, width):
    row_total = qkv_rows.shape[0]
    query_part = (
        head_norm(qkv_rows[:, :width].reshape(row_total, HEADS, HEAD_DIM))
        .astype(jnp.bfloat16)
        .reshape(row_total, width)
    )
    key_part = (
        head_norm(qkv_rows[:, width : 2 * width].reshape(row_total, HEADS, HEAD_DIM))
        .astype(jnp.bfloat16)
        .reshape(row_total, width)
    )
    value_part = qkv_rows[:, 2 * width :].astype(jnp.bfloat16)
    return (query_part, key_part, value_part)


def temporal_core(triple):
    query_part, key_part, value_part = triple
    all_frames, single, items, width = query_part.shape
    scale = HEAD_DIM ** (-0.5)
    query_heads = query_part.reshape(all_frames, items, HEADS, HEAD_DIM)
    key_heads = key_part.reshape(all_frames, items, HEADS, HEAD_DIM)
    value_heads = value_part.reshape(all_frames, items, HEADS, HEAD_DIM)
    scores = (
        jnp.einsum("fphd,gphd->phfg", query_heads, key_heads, preferred_element_type=jnp.float32)
        * scale
    )
    expo = jnp.exp(scores)
    total = jnp.sum(expo, axis=-1)
    numer = jnp.einsum(
        "phfg,gphd->fphd",
        expo.astype(jnp.bfloat16),
        value_heads,
        preferred_element_type=jnp.float32,
    )
    result = (numer / jnp.transpose(total, (2, 0, 1))[..., None]).astype(jnp.bfloat16)
    result = result.reshape(all_frames, single, items, width)
    return lax.all_to_all(result, "frame", split_axis=0, concat_axis=1, tiled=True)


def shards(
    spatial_queries,
    spatial_keys,
    spatial_values,
    hidden,
    spatial_out_weight,
    spatial_gain,
    temporal_qkv_weight,
    temporal_out_weight,
    temporal_gain,
    tile_list,
    tile_count,
):
    frames_here, tokens_here, width = spatial_queries.shape
    attended = spatial_attention(
        spatial_queries, spatial_keys, spatial_values, tile_list, tile_count
    )
    projected = jnp.dot(
        attended.reshape(frames_here * tokens_here, width),
        spatial_out_weight,
        preferred_element_type=jnp.float32,
    )
    mixed = (
        hidden.reshape(frames_here * tokens_here, D).astype(jnp.float32)
        + row_norm(projected, spatial_gain)
    ).astype(jnp.bfloat16)
    groups = lax.axis_size("frame")
    share = tokens_here // groups
    features = lax.all_to_all(
        mixed.reshape(frames_here, groups, share, D),
        "frame",
        split_axis=1,
        concat_axis=0,
        tiled=True,
    )
    all_frames, single, items, model_width = features.shape
    qkv_rows = jnp.dot(
        features.reshape(all_frames * items, model_width),
        temporal_qkv_weight,
        preferred_element_type=jnp.float32,
    )
    query_part, key_part, value_part = split_heads(qkv_rows, width)
    gathered = temporal_core(
        (
            query_part.reshape(all_frames, single, items, width),
            key_part.reshape(all_frames, single, items, width),
            value_part.reshape(all_frames, single, items, width),
        )
    )
    temporal_attended = gathered.reshape(frames_here * tokens_here, width)
    out_rows = jnp.dot(temporal_attended, temporal_out_weight, preferred_element_type=jnp.float32)
    block_out = (mixed.astype(jnp.float32) + row_norm(out_rows, temporal_gain)).astype(jnp.bfloat16)
    return block_out.reshape(frames_here, tokens_here, D)


def solution(mesh):
    placed = (
        P(("group", "frame"), "strip", None),
        P(("group", "frame"), "strip", None),
        P(("group", "frame"), "strip", None),
        P(("group", "frame"), "strip", None),
        P(),
        P(),
        P(),
        P(),
        P(),
        P(("group", "frame"), "strip", None),
        P(("group", "frame"), "strip"),
    )
    return jax.shard_map(
        shards,
        mesh=mesh,
        in_specs=placed,
        out_specs=P(("group", "frame"), "strip", None),
        check_vma=False,
    )
```

profile of v0, /device:TPU:0, one launch (start us, length us, event | category | flops | bytes accessed | tf_op | source)
XLA Modules:
  0.0 173.1 jit_solution(1938249493412843711)
XLA Ops:
  0.0 0.0 copy-start
  0.0 3.0 %convert_multiply_fusion.1 = f32[4,256,576]{1,2,0:T(8,128)} fusion(bf16[4,256,576]{1,2,0:T(8,128)(2,1)} %param.12), kind=kLoop, calls=%fused_computation.20 | loop fusion | flops 1179648 | bytes 3538944 | tf_op jit(solution)/shard_map/mul | solution.py:31
  3.0 1.9 %reduce_sum.72 = f32[4,256,8]{1,2,0:T(8,128)S(1)} reduce(f32[4,256,8,72]{1,3,2,0:T(8,128)} %bitcast.72, f32[]{:T(128)} %constant.9.clone.1), dimensions={3}, to_apply=%region_0.0 | reduce | flops 581632 | bytes 2392068 | tf_op jit(solution)/shard_map/reduce_sum | solution.py:31
  4.9 0.0 copy-start.5
  4.9 1.6 fusion.10
  6.5 0.0 copy-done.5
  6.5 0.0 copy-start.11
  6.5 1.8 %fusion.22 = (bf16[4,128,1152]{1,2,0:T(8,128)(2,1)}, bf16[4,128,1152]{1,2,0:T(8,128)(2,1)}) fusion(bf16[4,256,576]{1,2,0:T(8,128)(2,1)S(1)} %fusion.10, bf16[4,256,576]{1,2,0:T(8,128)(2,1)S(1)} %copy-done.5), kind=kLoop, calls=%fused_computation.35 | loop fusion | flops 4718592 | bytes 4718592 | tf_op jit(solution)/shard_map/concatenate | solution.py:48
  8.3 6.0 %collective-permute-start = (bf16[4,128,1152]{1,2,0:T(8,128)(2,1)}, bf16[4,128,1152]{1,2,0:T(8,128)(2,1)}, u32[]{:S(2)}, u32[]{:S(2)}) collective-permute-start(bf16[4,128,1152]{1,2,0:T(8,128)(2,1)} %get-tuple-element.11), channel_id=1, source_target_pairs={{0,1},{1,2},{2,3},{4,5},{5,6},{6,7},{8,9},{9,10},{10,11},{12,13},{... | collective-permute-start | bytes 3538952 | tf_op jit(solution)/shard_map/ppermute | solution.py:24
  14.3 1.3 collective-permute-start.1
  15.6 0.0 copy-done.10
  15.6 0.0 copy-done.11
  15.6 0.1 fusion.25
  15.8 0.1 broadcast_in_dim.2
  15.9 3.6 %reshape.133 = f32[4,2,128,8,72]{2,1,4,3,0:T(2,128)} reshape(bf16[4,256,576]{1,2,0:T(8,128)(2,1)} %param.11) | data formatting | bytes 3538944 | tf_op jit(solution)/shard_map/reshape | solution.py:43
  19.5 2.7 %multiply_reduce_fusion.2 = f32[4,2,128,8]{2,1,3,0:T(2,128)S(1)} fusion(f32[4,2,128,8,72]{2,1,4,3,0:T(2,128)} %reshape.133), kind=kLoop, calls=%fused_computation.29 | loop fusion | flops 1171456 | bytes 2392064 | tf_op jit(solution)/shard_map/reduce_sum | solution.py:31
  22.2 16.6 %collective-permute-done = bf16[4,128,1152]{1,2,0:T(8,128)(2,1)} collective-permute-done((bf16[4,128,1152]{1,2,0:T(8,128)(2,1)}, bf16[4,128,1152]{1,2,0:T(8,128)(2,1)}, u32[]{:S(2)}, u32[]{:S(2)}) %collective-permute-start) | collective-permute-done | bytes 1179680 | tf_op jit(solution)/shard_map/ppermute | solution.py:24
  38.8 5.1 %collective-permute-done.1 = bf16[4,128,1152]{1,2,0:T(8,128)(2,1)} collective-permute-done((bf16[4,128,1152]{1,2,0:T(8,128)(2,1)}, bf16[4,128,1152]{1,2,0:T(8,128)(2,1)}, u32[]{:S(2)}, u32[]{:S(2)}) %collective-permute-start.1) | collective-permute-done | bytes 1179680 | tf_op jit(solution)/shard_map/ppermute | solution.py:25
  43.9 0.0 copy-done.6
  43.9 1.9 %pad_maximum_fusion = bf16[4,512,1152]{1,2,0:T(8,128)(2,1)S(1)} fusion(bf16[4,128,1152]{1,2,0:T(8,128)(2,1)} %collective-permute-done.1, bf16[4,256,576]{1,2,0:T(8,128)(2,1)S(1)} %copy-done.6, bf16[4,256,576]{1,2,0:T(8,128)(2,1)S(1)} %fusion.10, bf16[4,128,1152]{1,2,0:T(8,128)(2,1)} %collective-permute-done), kind=kLoop, calls=%fused_computation.6 | loop fusion | flops 18874368 | bytes 9437184 | tf_op jit(solution)/shard_map/concatenate | solution.py:26
  45.8 0.0 copy-start.2
  45.8 0.3 fusion.28
  46.1 1.3 copy-done.2
  47.5 4.6 %fusion = (f32[4,2,8,128]{3,1,2,0:T(2,128)S(1)}, f32[4,8,512,2,128]{4,2,3,1,0:T(8,128)S(1)}) fusion(f32[4,2,512]{2,1,0:T(2,128)S(1)} %mul.133, bf16[4,512,8,72,1]{1,3,4,2,0:T(8,128)(2,1)S(1)} %bitcast.69, f32[4,2,128,8,72]{2,1,4,3,0:T(2,128)S(1)} %copy-done.2, f32[4,2,128,8]{2,1,3,0:T(2,128)S(1)} %add_rsqrt_fusion.2), kind=kOutput, calls=%fused_computation.1 | convolution fusion | flops 617734144 | bytes 21577728 | tf_op jit(solution)/shard_map/ftqhd,fkhd->fthqk/dot_general | solution.py:61
  52.1 3.7 %fusion.11 = bf16[4,2,128,8,72]{2,4,1,3,0:T(8,128)(2,1)S(1)} fusion(bf16[4,512,8,72,1]{1,3,4,2,0:T(8,128)(2,1)S(1)} %bitcast.76, f32[4,8,512,2,128]{4,2,3,1,0:T(8,128)S(1)} %get-tuple-element.14, f32[4,2,512]{2,1,0:T(2,128)S(1)} %mul.133, f32[4,2,128,8]{2,1,3,0:T(2,128)S(1)} %bitcast.81), kind=kOutput, calls=%fused_computation.26 | convolution fusion | flops 617742336 | bytes 20365312 | tf_op jit(solution)/shard_map/fthqk,fkhd->ftqhd/dot_general | solution.py:68
  55.8 1.1 copy.59
  56.8 1.7 reshape_reshape.6
  58.5 0.0 copy-done
  58.5 3.8 %multiply_reduce_fusion.1 = (f32[1024]{0:T(1024)S(1)}, f32[1024,1152]{1,0:T(8,128)S(1)}) fusion(bf16[1024,576]{0,1:T(8,128)(2,1)} %reshape_reshape.6, bf16[576,1152]{1,0:T(8,128)(2,1)S(1)} %copy-done), kind=kOutput, calls=%fused_computation.11 | convolution fusion | flops 1361312768 | bytes 7229440 | tf_op jit(solution)/shard_map/dot_general | solution.py:135
  62.3 0.0 copy-done.7
  62.3 0.0 copy-done.8
  62.3 0.9 fusion.6
  63.2 0.2 copy.60
  63.4 1.2 copy-done.3
  64.7 31.3 %all_to_all.30 = bf16[4,4,64,1152]{3,2,0,1:T(8,128)(2,1)S(1)} all-to-all(bf16[4,4,64,1152]{3,2,0,1:T(8,128)(2,1)S(1)} %copy.60), channel_id=1, replica_groups=mesh['group'=2,'frame'=4,'strip'=4] {'frame'}, dimensions={1} | all-to-all | bytes 4718592 | tf_op jit(solution)/shard_map/all_to_all | solution.py:146
  96.0 4.9 %fusion.29 = f32[1024,1728]{0,1:T(8,128)S(1)} fusion(bf16[1024,1152]{1,0:T(8,128)(2,1)S(1)} %bitcast.75, bf16[1152,1728]{0,1:T(8,128)(2,1)S(1)} %copy-done.12), kind=kOutput, calls=%fused_computation.54 | convolution fusion | flops 4076863488 | bytes 13418496 | tf_op jit(solution)/shard_map/dot_general | solution.py:154
  100.9 0.2 slice.45
  101.1 4.2 %slice_multiply_fusion.1 = (f32[1024,576]{0,1:T(8,128)}, f32[1024,576]{0,1:T(8,128)}, f32[1024,576]{0,1:T(8,128)}, f32[1024,576]{0,1:T(8,128)}) fusion(f32[1024,1728]{0,1:T(8,128)S(1)} %fusion.29), kind=kLoop, calls=%fused_computation.52 | loop fusion | flops 1179648 | bytes 14155776 | tf_op jit(solution)/shard_map/mul | solution.py:31
  105.2 2.7 %reshape.136 = bf16[16,64,8,72]{1,0,3,2:T(8,128)(2,1)} reshape(bf16[1024,576]{0,1:T(8,128)(2,1)S(1)} %slice.45) | data formatting | bytes 2359296 | tf_op jit(solution)/shard_map/reshape;reshape | solution.py:100
  108.0 5.4 %copy.68 = bf16[16,64,8,72]{3,0,2,1:T(8,128)(2,1)S(1)} copy(bf16[16,64,8,72]{1,0,3,2:T(8,128)(2,1)} %reshape.136) | data formatting | bytes 2359296 | tf_op jit(solution)/shard_map/reshape;reshape | solution.py:100
  113.3 1.9 %reduce_sum.76 = f32[1024,8]{0,1:T(8,128)S(1)} reduce(f32[1024,8,72]{0,2,1:T(8,128)} %bitcast.71, f32[]{:T(128)} %constant.9.clone.1), dimensions={2}, to_apply=%region_5.0 | reduce | flops 581632 | bytes 2392068 | tf_op jit(solution)/shard_map/reduce_sum | solution.py:31
  115.3 1.9 %reduce_sum.77 = f32[1024,8]{0,1:T(8,128)S(1)} reduce(f32[1024,8,72]{0,2,1:T(8,128)} %bitcast.70, f32[]{:T(128)} %constant.9.clone.1), dimensions={2}, to_apply=%region_6.0 | reduce | flops 581632 | bytes 2392068 | tf_op jit(solution)/shard_map/reduce_sum | solution.py:31
  117.3 0.2 copy.80
  117.5 0.2 copy.79
  117.7 3.2 %copy.64 = f32[1024,576]{1,0:T(8,128)} copy(f32[1024,576]{0,1:T(8,128)} %get-tuple-element.7) | data formatting | bytes 4718592 | tf_op jit(solution)/shard_map/slice | solution.py:86
  120.9 5.3 %reshape.127 = f32[16,64,8,72]{3,2,1,0:T(8,128)} reshape(f32[1024,576]{1,0:T(8,128)} %copy.64) | data formatting | bytes 4718592 | tf_op jit(solution)/shard_map/reshape | solution.py:86
  126.1 3.2 %copy.62 = f32[1024,576]{1,0:T(8,128)} copy(f32[1024,576]{0,1:T(8,128)} %get-tuple-element.8) | data formatting | bytes 4718592 | tf_op jit(solution)/shard_map/slice | solution.py:81
  129.4 5.3 %reshape.126 = f32[16,64,8,72]{3,2,1,0:T(8,128)} reshape(f32[1024,576]{1,0:T(8,128)} %copy.62) | data formatting | bytes 4718592 | tf_op jit(solution)/shard_map/reshape | solution.py:81
  134.6 6.0 %multiply_convert_fusion = (bf16[16,64,8,72]{3,2,1,0:T(8,128)(2,1)S(1)}, bf16[16,64,8,72]{3,2,1,0:T(8,128)(2,1)S(1)}) fusion(f32[16,64,8,72]{3,2,1,0:T(8,128)} %reshape.127, f32[16,64,8]{2,1,0:T(8,128)S(1)} %bitcast.77, f32[16,64,8,72]{3,2,1,0:T(8,128)} %reshape.126, f32[16,64,8]{2,1,0:T(8,128)S(1)} %bitcast.78), kind=kLoop, calls=%fused_computation.15 | loop fusion | flops 2359296 | bytes 7143424 | tf_op jit(solution)/shard_map/convert_element_type | solution.py:87
  140.7 3.5 %fusion.8 = (f32[64,8,16]{2,1,0:T(8,128)S(1)}, f32[64,8,16,16]{2,3,1,0:T(8,128)S(1)}) fusion(bf16[16,64,8,72]{3,2,1,0:T(8,128)(2,1)S(1)} %get-tuple-element.21, bf16[16,64,8,72]{3,2,1,0:T(8,128)(2,1)S(1)} %get-tuple-element.22), kind=kOutput, calls=%fused_computation.17 | convolution fusion | flops 19128320 | bytes 2916352 | tf_op jit(solution)/shard_map/fphd,gphd->phfg/dot_general | solution.py:102
  144.1 2.2 %fusion.7 = bf16[16,64,8,72]{3,0,2,1:T(8,128)(2,1)S(1)} fusion(bf16[16,64,8,72]{3,0,2,1:T(8,128)(2,1)S(1)} %copy.68, f32[64,8,16,16]{2,3,1,0:T(8,128)S(1)} %get-tuple-element.18, f32[16,64,8]{0,2,1:T(8,128)S(1)} %bitcast.80), kind=kOutput, calls=%fused_computation.13 | convolution fusion | flops 20316160 | bytes 2916352 | tf_op jit(solution)/shard_map/phfg,gphd->fphd/dot_general | solution.py:107
  146.4 0.5 copy.70
  146.9 1.7 reshape.128
  148.6 0.0 copy-start.13
  148.6 19.8 %all_to_all.31 = bf16[16,1,64,576]{3,2,1,0:T(8,128)(2,1)S(1)} all-to-all(bf16[16,1,64,576]{3,2,1,0:T(8,128)(2,1)S(1)} %bitcast.73), channel_id=1, replica_groups=mesh['group'=2,'frame'=4,'strip'=4] {'frame'}, dimensions={0} | all-to-all | bytes 2359296 | tf_op jit(solution)/shard_map/all_to_all | solution.py:115
  168.4 0.1 copy.72
  168.6 0.0 copy-done.13
  168.6 0.0 copy-start.4
  168.6 0.0 copy-start.9
  168.6 2.2 %multiply_reduce_fusion = (f32[1024]{0:T(1024)S(1)}, f32[1024,1152]{1,0:T(8,128)S(1)}) fusion(bf16[1024,576]{1,0:T(8,128)(2,1)S(1)} %bitcast.79, bf16[576,1152]{1,0:T(8,128)(2,1)S(1)} %copy-done.13), kind=kOutput, calls=%fused_computation.10 | convolution fusion | flops 1361312768 | bytes 7229440 | tf_op jit(solution)/shard_map/dot_general | solution.py:168
  170.8 0.0 copy-done.4
  170.8 0.0 copy-done.9
  170.9 0.0 copy-start.1
  170.9 2.2 %add_convert_fusion = bf16[1024,1152]{1,0:T(8,128)(2,1)} fusion(f32[1024,1152]{1,0:T(8,128)S(1)} %get-tuple-element.20, bf16[1024,1152]{1,0:T(8,128)(2,1)S(1)} %copy-done.4, f32[1152]{0:T(1024)S(1)} %copy-done.9, f32[1024]{0:T(1024)S(1)} %add_rsqrt_fusion.4), kind=kLoop, calls=%fused_computation.9 | loop fusion | flops 5898240 | bytes 9445888 | tf_op jit(solution)/shard_map/convert_element_type | solution.py:169
  (20 shorter events, 0.1 us)
Async XLA Ops:
  0.0 58.5 %copy-start = (bf16[576,1152]{1,0:T(8,128)(2,1)S(1)}, bf16[576,1152]{1,0:T(8,128)(2,1)}, u32[]{:S(2)}) copy-start(bf16[576,1152]{1,0:T(8,128)(2,1)} %param.15) | copy-start | bytes 3981316
  4.9 1.6 copy-start.5
  6.5 9.1 %copy-start.10 = (s32[4,2,3]{0,1,2:T(2,128)S(1)}, s32[4,2,3]{0,1,2:T(2,128)}, u32[]{:S(2)}) copy-start(s32[4,2,3]{0,1,2:T(2,128)} %param.20) | copy-start | bytes 292
  6.5 9.1 %copy-start.11 = (s32[4,2]{0,1:T(2,128)S(1)}, s32[4,2]{0,1:T(2,128)}, u32[]{:S(2)}) copy-start(s32[4,2]{0,1:T(2,128)} %param.21) | copy-start | bytes 100
  8.3 30.5 %collective-permute-start = (bf16[4,128,1152]{1,2,0:T(8,128)(2,1)}, bf16[4,128,1152]{1,2,0:T(8,128)(2,1)}, u32[]{:S(2)}, u32[]{:S(2)}) collective-permute-start(bf16[4,128,1152]{1,2,0:T(8,128)(2,1)} %get-tuple-element.11), channel_id=1, source_target_pairs={{0,1},{1,2},{2,3},{4,5},{5,6},{6,7},{8,9},{9,10},{10,11},{12,13},{... | collective-permute-start | bytes 3538952 | tf_op jit(solution)/shard_map/ppermute | solution.py:24
  14.3 29.6 %collective-permute-start.1 = (bf16[4,128,1152]{1,2,0:T(8,128)(2,1)}, bf16[4,128,1152]{1,2,0:T(8,128)(2,1)}, u32[]{:S(2)}, u32[]{:S(2)}) collective-permute-start(bf16[4,128,1152]{1,2,0:T(8,128)(2,1)} %get-tuple-element.12), channel_id=1, source_target_pairs={{1,0},{2,1},{3,2},{5,4},{6,5},{7,6},{9,8},{10,9},{11,10},{13,12},{... | collective-permute-start | bytes 3538952 | tf_op jit(solution)/shard_map/ppermute | solution.py:25
  19.5 24.5 %copy-start.6 = (bf16[4,256,576]{1,2,0:T(8,128)(2,1)S(1)}, bf16[4,256,576]{1,2,0:T(8,128)(2,1)}, u32[]{:S(2)}) copy-start(bf16[4,256,576]{1,2,0:T(8,128)(2,1)} %param.13) | copy-start | bytes 3538948
  45.8 1.7 copy-start.2
  58.5 3.8 %copy-start.7 = (bf16[4,256,1152]{2,1,0:T(8,128)(2,1)S(1)}, bf16[4,256,1152]{2,1,0:T(8,128)(2,1)}, u32[]{:S(2)}) copy-start(bf16[4,256,1152]{2,1,0:T(8,128)(2,1)} %param.14) | copy-start | bytes 7077892
  58.5 3.8 %copy-start.8 = (f32[1152]{0:T(1024)S(1)}, f32[1152]{0:T(1024)}, u32[]{:S(2)}) copy-start(f32[1152]{0:T(1024)} %param.16) | copy-start | bytes 13828
  63.2 1.5 copy-start.3
  64.7 31.3 %copy-start.12 = (bf16[1152,1728]{0,1:T(8,128)(2,1)S(1)}, bf16[1152,1728]{0,1:T(8,128)(2,1)}, u32[]{:S(2)}) copy-start(bf16[1152,1728]{0,1:T(8,128)(2,1)} %param.17) | copy-start | bytes 11943940
  148.6 19.9 %copy-start.13 = (bf16[576,1152]{1,0:T(8,128)(2,1)S(1)}, bf16[576,1152]{1,0:T(8,128)(2,1)}, u32[]{:S(2)}) copy-start(bf16[576,1152]{1,0:T(8,128)(2,1)} %param.18) | copy-start | bytes 3981316
  168.6 2.3 %copy-start.4 = (bf16[1024,1152]{1,0:T(8,128)(2,1)S(1)}, bf16[1024,1152]{1,0:T(8,128)(2,1)}, u32[]{:S(2)}) copy-start(bf16[1024,1152]{1,0:T(8,128)(2,1)} %copy-done.3) | copy-start | bytes 7077892
  168.6 2.3 %copy-start.9 = (f32[1152]{0:T(1024)S(1)}, f32[1152]{0:T(1024)}, u32[]{:S(2)}) copy-start(f32[1152]{0:T(1024)} %param.19) | copy-start | bytes 13828
  170.9 2.2 %copy-start.1 = (bf16[576,1152]{1,0:T(8,128)(2,1)S(1)}, bf16[576,1152]{1,0:T(8,128)(2,1)}, u32[]{:S(2)}) copy-start(bf16[576,1152]{1,0:T(8,128)(2,1)} %param.15) | copy-start | bytes 3981316
where the time goes:
time: 174 us; the launch traced here: 173 us
  blocking collectives  51.1 us (29%)
  local copies, waits for them, and re-layouts  37.6 us (22%)
  other arithmetic  30.2 us (17%)
  matrix products  24.8 us (14%)
  waiting for transfers between devices  21.7 us (12%)
  starting transfers between devices  7.23 us (4%)
    all_to_all x1, blocking collectives, shards(): lax.all_to_all(mixed.reshape(frames_here, groups, share, D), 'frame', spl...  31.3 us
    all_to_all x1, blocking collectives, temporal_core(): lax.all_to_all(result, 'frame', split_axis=0, concat_axis=1, tiled=True)  19.8 us
    ppermute x1, waiting for transfers between devices, with_halo(): before = lax.ppermute(last, axis, up)  16.6 us
    reduce_sum x4, other arithmetic, head_norm(): jnp.mean(values * values, axis=-1, keepdims=True) + epsilon  8.42 us
    another operation x2, local copies, waits for them, and re-layouts, temporal_core(): value_heads = value_part.reshape(all_frames, items, HEADS, HEAD_DIM)  8.11 us
    mul x2, other arithmetic, head_norm(): values * values  7.14 us
    convert_element_type x1, other arithmetic, split_heads(): key_part = head_norm(qkv_rows[:, width:2 * width].reshape(row_total, HEAD...  6.02 us
    ppermute x1, starting transfers between devices, with_halo(): before = lax.ppermute(last, axis, up)  5.95 us
  transfers between devices with their start and end apart: 2, of which 2 were waited for; matrix products, arithmetic and copies ran while one was open for 4% of the time, Pallas kernels for 0%

commit v1 on v0

v1 whole, which is shorter than its diff:
```python
import functools
import math

import jax
import jax.numpy as jnp
from jax import lax
from jax.experimental import pallas as pl
from jax.experimental.pallas import tpu as pltpu
from jax.sharding import PartitionSpec as P

HEAD_DIM = 72
HEADS = 8
TILE = 128
MAXT = 3
SUB = 16
EPS = 1e-06
EXP2_SCALE = HEAD_DIM ** -0.5 * math.log2(math.e)

BF = jnp.bfloat16
F32 = jnp.float32


def peer(i, j, n):
    return i ^ j if n & (n - 1) == 0 else (i + j) % n


def vmem(limit):
    return pltpu.CompilerParams(vmem_limit_bytes=limit << 20)


def whole(shape):
    return pl.BlockSpec(shape, lambda *_: (0,) * len(shape))


def contract(a, b, da, db):
    return lax.dot_general(a, b, (((da,), (db,)), ((), ())), preferred_element_type=F32)


def head_scale(x):
    return lax.rsqrt(jnp.mean(x * x, axis=0, keepdims=True) + EPS)


def head(h, base=0):
    return slice(base + h * HEAD_DIM, base + (h + 1) * HEAD_DIM)


def prep_kernel(info, k_ref, v_ref, a_ref, b_ref, scratch):
    width = k_ref.shape[1]
    for h in range(width // HEAD_DIM):
        x = k_ref[0, head(h), :].astype(F32)
        scratch[head(h), :] = (x * head_scale(x)).astype(BF)
    even = info[1] % 2 == 0

    def fill(first, second):
        first[:width, :] = scratch[:, :TILE]
        first[width:, :] = v_ref[0, :, :TILE]
        second[:width, :] = scratch[:, TILE:]
        second[width:, :] = v_ref[0, :, TILE:]

    @pl.when(even)
    def _():
        fill(b_ref, a_ref)

    @pl.when(jnp.logical_not(even))
    def _():
        fill(a_ref, b_ref)


def spatial_kernel(frame, n_groups, info, q_ref, a_ref, b_ref, ra_ref, rb_ref, h_ref, w_ref, g_ref, *rest):
    outs, (kv, att, mix) = rest[:n_groups], rest[n_groups:]
    width, tokens = q_ref.shape[1], q_ref.shape[2]
    tiles = tokens // TILE
    share = tokens // n_groups
    for i, ref in enumerate((a_ref, b_ref, ra_ref, rb_ref)):
        kv[:, i * TILE:(i + 1) * TILE] = ref[...]
    strip = info[1]
    odd = strip % 2
    first = strip * tiles
    places = (first + 1 - odd, first + odd, first + 2 - 3 * odd, first - 1 + 3 * odd)
    frames = info_frames(info, tiles)
    base = 2 + frames * tiles
    masks = []
    for t in range(tiles):
        row = frame * tiles + t
        live = info[2 + row]
        cells = []
        for place in places:
            hit = jnp.bool_(False)
            for j in range(MAXT):
                hit = hit | ((info[base + row * MAXT + j] == place) & (j < live))
            cells.append(jnp.where(hit, 1.0, 0.0).astype(F32))
        masks.append(cells)
    for h in range(width // HEAD_DIM):
        q = q_ref[0, head(h), :].astype(F32)
        qn = (q * (head_scale(q) * EXP2_SCALE)).astype(BF)
        s = contract(kv[head(h), :], qn, 0, 0)
        p = jnp.exp2(s)
        p = jnp.concatenate(
            [
                jnp.concatenate(
                    [
                        p[i * TILE:(i + 1) * TILE, t * TILE:(t + 1) * TILE] * masks[t][i]
                        for t in range(tiles)
                    ],
                    axis=1,
                )
                for i in range(4)
            ],
            axis=0,
        )
        total = jnp.sum(p, axis=0, keepdims=True)
        o = contract(kv[head(h, width), :], p.astype(BF), 1, 0)
        att[head(h), :] = (o / total).astype(BF)
    proj = contract(att[...], w_ref[...], 0, 0)
    scale = lax.rsqrt(jnp.mean(proj * proj, axis=-1, keepdims=True) + EPS)
    mix[...] = (h_ref[0].astype(F32) + proj * scale * g_ref[...]).astype(BF)
    for j, out in enumerate(outs):
        group = peer(info[0], j, n_groups)
        out[...] = mix[pl.ds(pl.multiple_of(group * share, SUB), share), :]


def info_frames(info, tiles):
    return (info.shape[0] - 2) // (tiles * (1 + MAXT))


def rel_order(c, n_groups):
    return [j ^ (c & 1) for j in range(n_groups)] if n_groups % 2 == 0 else list(range(n_groups))


def temporal_kernel(n_groups, frames, *refs):
    n_in = n_groups * frames
    pieces, w_ref = refs[:n_in], refs[n_in]
    outs = refs[n_in + 1:n_in + 1 + n_groups]
    x, qkv, att = refs[n_in + 1 + n_groups:]
    chunks = pieces[0].shape[0] // SUB
    rows = n_in * SUB
    width = w_ref.shape[0] // 3
    row_pos = lax.broadcasted_iota(jnp.int32, (rows, rows), 0) % SUB
    col_pos = lax.broadcasted_iota(jnp.int32, (rows, rows), 1) % SUB
    same = jnp.where(row_pos == col_pos, 1.0, 0.0).astype(F32)
    for c in range(chunks):
        order = rel_order(c, n_groups)
        for slot, j in enumerate(order):
            for f in range(frames):
                at = (slot * frames + f) * SUB
                x[c, at:at + SUB, :] = pieces[j * frames + f][c * SUB:(c + 1) * SUB, :]
        qkv[c] = contract(w_ref[...], x[c], 1, 1)
        for h in range(width // HEAD_DIM):
            q = qkv[c, head(h), :]
            k = qkv[c, head(h, width), :]
            v = qkv[c, head(h, 2 * width), :].astype(BF)
            qn = (q * (head_scale(q) * EXP2_SCALE)).astype(BF)
            kn = (k * head_scale(k)).astype(BF)
            p = jnp.exp2(contract(kn, qn, 0, 0)) * same
            total = jnp.sum(p, axis=0, keepdims=True)
            o = contract(v, p.astype(BF), 1, 0)
            att[c, head(h), :] = (o / total).astype(BF)
    lanes = frames * SUB
    if chunks == 2 and n_groups % 2 == 0:
        low = lax.broadcasted_iota(jnp.int32, (width, 2 * lanes), 1) < lanes
        for m in range(n_groups // 2):
            one = att[0, :, 2 * lanes * m:2 * lanes * (m + 1)]
            two = att[1, :, 2 * lanes * m:2 * lanes * (m + 1)]
            outs[2 * m][...] = jnp.where(low, one, two)
            outs[2 * m + 1][...] = jnp.where(low, two, one)
    else:
        for c in range(chunks):
            for slot, j in enumerate(rel_order(c, n_groups)):
                outs[j][:, c * lanes:(c + 1) * lanes] = att[c, :, slot * lanes:(slot + 1) * lanes]


def output_kernel(n_groups, frames, half, halves, aliased, info, *refs):
    n_in = n_groups * frames
    atts, pieces = refs[:n_groups], refs[n_groups:n_groups + n_in]
    w_ref, g_ref = refs[n_groups + n_in:n_groups + n_in + 2]
    rest = refs[n_groups + n_in + 2 + aliased:]
    out, buf, sems = rest
    rows = pieces[0].shape[0]
    chunks = rows // SUB
    merged = chunks == 2 and n_groups % 2 == 0
    copies = []
    for j in range(n_groups):
        proj = contract(atts[j][...], w_ref[...], 0, 0)
        scale = lax.rsqrt(jnp.mean(proj * proj, axis=-1, keepdims=True) + EPS)
        res = proj * scale * g_ref[...]
        for slot in range(chunks):
            c = slot ^ (j & 1) if merged else slot
            for f in range(frames):
                at = (slot * frames + f) * SUB
                mine = pieces[j * frames + f][c * SUB:(c + 1) * SUB, :].astype(F32)
                buf[j, f, c * SUB:(c + 1) * SUB, :] = (mine + res[at:at + SUB, :]).astype(BF)
        group = peer(info[0], j, n_groups)
        start = pl.multiple_of((group * halves + half) * rows, SUB)
        copy = pltpu.make_async_copy(buf.at[j], out.at[:, pl.ds(start, rows), :], sems.at[j])
        copy.start()
        copies.append(copy)
    for copy in copies:
        copy.wait()


def shards(
    spatial_queries,
    spatial_keys,
    spatial_values,
    hidden,
    spatial_out_weight,
    spatial_gain,
    temporal_qkv_weight,
    temporal_out_weight,
    temporal_gain,
    tile_list,
    tile_count,
):
    frames, tokens, width = spatial_queries.shape
    model = hidden.shape[2]
    groups = lax.axis_size("frame")
    strips = lax.axis_size("strip")
    share = tokens // groups
    halves = 2 if share % (4 * SUB) == 0 else 1
    rows = share // halves
    queries = jnp.transpose(spatial_queries, (0, 2, 1))
    keys = jnp.transpose(spatial_keys, (0, 2, 1))
    values = jnp.transpose(spatial_values, (0, 2, 1))
    qkv_weight = temporal_qkv_weight.T
    gain_one = spatial_gain.reshape(1, model)
    gain_two = temporal_gain.reshape(1, model)
    me, strip = lax.axis_index("frame"), lax.axis_index("strip")
    info = jnp.concatenate(
        [jnp.stack([me, strip]).astype(jnp.int32), tile_count.reshape(-1), tile_list.reshape(-1)]
    )
    near = [(i, i ^ 1) for i in range(strips) if i ^ 1 < strips]
    far = [e for i in range(1, strips - 1, 2) for e in ((i, i + 1), (i + 1, i))]
    edge = jax.ShapeDtypeStruct((2 * width, TILE), BF)

    tiles_out, halos = [], []
    for f in range(frames):
        frame_block = pl.BlockSpec((1, width, tokens), lambda i, _, f=f: (f, 0, 0))
        a, b = pl.pallas_call(
            prep_kernel,
            grid_spec=pltpu.PrefetchScalarGridSpec(
                num_scalar_prefetch=1,
                grid=(1,),
                in_specs=[frame_block, frame_block],
                out_specs=[whole(edge.shape)] * 2,
                scratch_shapes=[pltpu.VMEM((width, tokens), BF)],
            ),
            out_shape=[edge, edge],
            compiler_params=vmem(16),
            name="prep",
        )(info, keys, values)
        tiles_out.append((a, b))
        halos.append((lax.ppermute(a, "strip", near), lax.ppermute(b, "strip", far)))

    mixed = [[None] * frames for _ in range(groups)]
    there = [[None] * frames for _ in range(groups)]
    for f in range(frames):
        frame_block = pl.BlockSpec((1, width, tokens), lambda i, _, f=f: (f, 0, 0))
        row_block = pl.BlockSpec((1, tokens, model), lambda i, _, f=f: (f, 0, 0))
        parts = pl.pallas_call(
            functools.partial(spatial_kernel, f, groups),
            grid_spec=pltpu.PrefetchScalarGridSpec(
                num_scalar_prefetch=1,
                grid=(1,),
                in_specs=[frame_block]
                + [whole(edge.shape)] * 4
                + [row_block, whole((width, model)), whole((1, model))],
                out_specs=[whole((share, model))] * groups,
                scratch_shapes=[
                    pltpu.VMEM((2 * width, 4 * TILE), BF),
                    pltpu.VMEM((width, tokens), BF),
                    pltpu.VMEM((tokens, model), BF),
                ],
            ),
            out_shape=[jax.ShapeDtypeStruct((share, model), BF)] * groups,
            compiler_params=vmem(32),
            name="spatial",
        )(info, queries, *tiles_out[f], *halos[f], hidden, spatial_out_weight, gain_one)
        for j in range(groups):
            mixed[j][f] = parts[j]
            pairs = [(i, peer(i, j, groups)) for i in range(groups)]
            there[j][f] = parts[j] if j == 0 else lax.ppermute(parts[j], "frame", pairs)

    out = None
    returned = []
    chunks = rows // SUB
    lanes = frames * SUB
    block = groups * frames * SUB
    here = [there[j][f] for j in range(groups) for f in range(frames)]
    mine = [mixed[j][f] for j in range(groups) for f in range(frames)]
    for half in range(halves):
        piece = pl.BlockSpec((rows, model), lambda *_, half=half: (half, 0))
        back = pl.pallas_call(
            functools.partial(temporal_kernel, groups, frames),
            grid=(1,),
            in_specs=[piece] * len(here) + [whole((3 * width, model))],
            out_specs=[whole((width, chunks * lanes))] * groups,
            out_shape=[jax.ShapeDtypeStruct((width, chunks * lanes), BF)] * groups,
            scratch_shapes=[
                pltpu.VMEM((chunks, block, model), BF),
                pltpu.VMEM((chunks, 3 * width, block), F32),
                pltpu.VMEM((chunks, width, block), BF),
            ],
            compiler_params=vmem(48),
            name="temporal",
        )(*here, qkv_weight)
        got = []
        for j in range(groups):
            pairs = [(peer(i, j, groups), i) for i in range(groups)]
            got.append(back[j] if j == 0 else lax.ppermute(back[j], "frame", pairs))
        returned.append(got)
    for half in range(halves):
        piece = pl.BlockSpec((rows, model), lambda *_, half=half: (half, 0))
        extra = [] if out is None else [out]
        any_spec = pl.BlockSpec(memory_space=pl.ANY)
        out = pl.pallas_call(
            functools.partial(output_kernel, groups, frames, half, halves, len(extra)),
            grid_spec=pltpu.PrefetchScalarGridSpec(
                num_scalar_prefetch=1,
                grid=(1,),
                in_specs=[whole((width, chunks * lanes))] * groups
                + [piece] * len(mine)
                + [whole((width, model)), whole((1, model))]
                + [any_spec] * len(extra),
                out_specs=any_spec,
                scratch_shapes=[
                    pltpu.VMEM((groups, frames, rows, model), BF),
                    pltpu.SemaphoreType.DMA((groups,)),
                ],
            ),
            out_shape=jax.ShapeDtypeStruct((frames, tokens, model), BF),
            input_output_aliases={1 + groups + len(mine) + 2: 0} if extra else {},
            compiler_params=vmem(32),
            name="output",
        )(info, *returned[half], *mine, temporal_out_weight, gain_two, *extra)
    return out


def solution(mesh):
    rows = P(("group", "frame"), "strip", None)
    placed = (rows, rows, rows, rows, P(), P(), P(), P(), P(), rows, P(("group", "frame"), "strip"))
    return jax.shard_map(shards, mesh=mesh, in_specs=placed, out_specs=rows, check_vma=False)
```

time: 174 us -> 96 us (0.55)
  blocking collectives: 51.1 us -> 0 us
  Pallas kernels: 0 us -> 45.1 us
  local copies, waits for them, and re-layouts: 37.6 us -> 4.3 us
  other arithmetic: 30.2 us -> 0.08 us
  matrix products: 24.8 us -> 0 us
  starting transfers between devices: 7.23 us -> 28.4 us
  waiting for transfers between devices: 21.7 us -> 16.5 us
    all_to_all x2 -> x0, blocking collectives: 51.1 us -> none  [the longest x1 31.3 us: shards(): lax.all_to_all(mixed.reshape(frames_here, groups, share, D), 'frame', spl...]
    pallas_call x0 -> x12, Pallas kernels: none -> 45.1 us  [the longest x2 20.8 us: shards(): pl.pallas_call(functools.partial(temporal_kernel, groups, frames), grid=(...]
    dot_general x7 -> x0, matrix products: 24.8 us -> none  [the longest x1 4.89 us: shards(): jnp.dot(features.reshape(all_frames * items, model_width), temporal_qkv_w...]
    ppermute x2 -> x26, starting transfers between devices: 7.23 us -> 28.4 us  [the longest x4 13 us: shards(): lax.ppermute(a, 'strip', near)]
    reshape x5 -> x4, local copies, waits for them, and re-layouts: 16 us -> 0.18 us  [the longest x1 0.09 us: shards(): tile_list.reshape(-1)]
    convert_element_type x5 -> x0, other arithmetic: 10.7 us -> none  [the longest x1 6.02 us: split_heads(): key_part = head_norm(qkv_rows[:, width:2 * width].reshape(row_total, HEAD...]
    another operation x3 -> x0, local copies, waits for them, and re-layouts: 9.77 us -> none  [the longest x2 8.11 us: temporal_core(): value_heads = value_part.reshape(all_frames, items, HEADS, HEAD_DIM)]
    reduce_sum x4 -> x0, other arithmetic: 8.42 us -> none  [head_norm(): jnp.mean(values * values, axis=-1, keepdims=True) + epsilon]
  transfers between devices with their start and end apart: 2 -> 26, of which waited for: 2 -> 8; matrix products, arithmetic and copies ran while one was open for 4% -> 0% of each run, Pallas kernels for 0% -> 33%
where the time goes in v1:
time: 96 us; the launch traced here: 94.8 us
  Pallas kernels  45.1 us (47%)
  starting transfers between devices  28.4 us (30%)
  waiting for transfers between devices  16.5 us (17%)
  local copies, waits for them, and re-layouts  4.3 us (4%)
    pallas_call x2, Pallas kernels, shards(): pl.pallas_call(functools.partial(temporal_kernel, groups, frames), grid=(...  20.8 us
    pallas_call x4, Pallas kernels, shards(): pl.pallas_call(functools.partial(spatial_kernel, f, groups), grid_spec=pl...  15.8 us
    ppermute x4, starting transfers between devices, shards(): lax.ppermute(a, 'strip', near)  13 us
    ppermute x12, waiting for transfers between devices, shards(): there[j][f] = parts[j] if j == 0 else lax.ppermute(parts[j], 'frame', pairs)  11.2 us
    ppermute x12, starting transfers between devices, shards(): there[j][f] = parts[j] if j == 0 else lax.ppermute(parts[j], 'frame', pairs)  8.6 us
    pallas_call x2, Pallas kernels, shards(): pl.pallas_call(functools.partial(output_kernel, groups, frames, half, hal...  5.57 us
    ppermute x6, starting transfers between devices, shards(): got.append(back[j] if j == 0 else lax.ppermute(back[j], 'frame', pairs))  4.17 us
    unnamed x18, local copies, waits for them, and re-layouts  4.12 us
  transfers between devices with their start and end apart: 26, of which 8 were waited for; matrix products, arithmetic and copies ran while one was open for 0% of the time, Pallas kernels for 33%

profile of v1, /device:TPU:0, one launch (start us, length us, event | category | flops | bytes accessed | tf_op | source)
XLA Modules:
  0.0 94.8 jit_solution(11557636546307371193)
XLA Ops:
  0.0 0.8 copy.15
  0.8 0.1 reshape.12
  0.9 0.8 copy.16
  1.6 0.1 reshape.13
  1.7 0.1 pad_add_fusion.info
  1.8 1.3 %copy-done.2 = bf16[4,256,576]{1,2,0:T(8,128)(2,1)S(1)} copy-done((bf16[4,256,576]{1,2,0:T(8,128)(2,1)S(1)}, bf16[4,256,576]{1,2,0:T(8,128)(2,1)}, u32[]{:S(2)}) %copy-start.2) | copy-done | bytes 1179672
  3.1 1.3 %copy-done.3 = bf16[4,256,576]{1,2,0:T(8,128)(2,1)S(1)} copy-done((bf16[4,256,576]{1,2,0:T(8,128)(2,1)S(1)}, bf16[4,256,576]{1,2,0:T(8,128)(2,1)}, u32[]{:S(2)}) %copy-start.3) | copy-done | bytes 1179672
  4.3 0.7 prep.7
  5.1 3.1 %collective-permute-start.6 = (bf16[1152,128]{1,0:T(8,128)(2,1)S(1)}, bf16[1152,128]{1,0:T(8,128)(2,1)S(1)}, u32[]{:S(2)}, u32[]{:S(2)}) collective-permute-start(bf16[1152,128]{1,0:T(8,128)(2,1)S(1)} %get-tuple-element.46.a_ref), channel_id=1, source_target_pairs={{0,1},{1,0},{2,3},{3,2},{4,5},{5,4},{6,7},{7,6},{8,9},{9,8},{10,11... | collective-permute-start | bytes 884744 | tf_op jit(solution)/shard_map/ppermute | solution.py:252
  8.2 0.7 collective-permute-start.7
  8.9 0.0 copy-start.4
  8.9 0.7 prep.6
  9.6 4.4 %collective-permute-start.4 = (bf16[1152,128]{1,0:T(8,128)(2,1)S(1)}, bf16[1152,128]{1,0:T(8,128)(2,1)S(1)}, u32[]{:S(2)}, u32[]{:S(2)}) collective-permute-start(bf16[1152,128]{1,0:T(8,128)(2,1)S(1)} %get-tuple-element.43.a_ref), channel_id=1, source_target_pairs={{0,1},{1,0},{2,3},{3,2},{4,5},{5,4},{6,7},{7,6},{8,9},{9,8},{10,11... | collective-permute-start | bytes 884744 | tf_op jit(solution)/shard_map/ppermute | solution.py:252
  14.1 0.7 collective-permute-start.5
  14.8 0.0 copy-start.1
  14.8 0.7 prep.5
  15.5 0.0 copy-start.6
  15.5 0.0 copy-start
  15.5 1.3 %collective-permute-start.2 = (bf16[1152,128]{1,0:T(8,128)(2,1)S(1)}, bf16[1152,128]{1,0:T(8,128)(2,1)S(1)}, u32[]{:S(2)}, u32[]{:S(2)}) collective-permute-start(bf16[1152,128]{1,0:T(8,128)(2,1)S(1)} %get-tuple-element.40.a_ref), channel_id=1, source_target_pairs={{0,1},{1,0},{2,3},{3,2},{4,5},{5,4},{6,7},{7,6},{8,9},{9,8},{10,11... | collective-permute-start | bytes 884744 | tf_op jit(solution)/shard_map/ppermute | solution.py:252
  16.9 0.0 collective-permute-done.6.ra_ref
  16.9 0.7 collective-permute-start.3
  17.5 0.7 prep.4
  18.3 0.0 collective-permute-done.7.rb_ref
  18.3 4.1 %collective-permute-start = (bf16[1152,128]{1,0:T(8,128)(2,1)S(1)}, bf16[1152,128]{1,0:T(8,128)(2,1)S(1)}, u32[]{:S(2)}, u32[]{:S(2)}) collective-permute-start(bf16[1152,128]{1,0:T(8,128)(2,1)S(1)} %get-tuple-element.37.a_ref), channel_id=1, source_target_pairs={{0,1},{1,0},{2,3},{3,2},{4,5},{5,4},{6,7},{7,6},{8,9},{9,8},{10,11... | collective-permute-start | bytes 884744 | tf_op jit(solution)/shard_map/ppermute | solution.py:252
  22.4 0.0 collective-permute-done.4.ra_ref
  22.4 0.7 collective-permute-start.1
  23.1 3.9 %spatial.7 = (bf16[64,1152]{1,0:T(8,128)(2,1)S(1)}, bf16[64,1152]{1,0:T(8,128)(2,1)S(1)}, bf16[64,1152]{1,0:T(8,128)(2,1)S(1)}, bf16[64,1152]{1,0:T(8,128)(2,1)S(1)}) custom-call(s32[34]{0:T(128)S(1)} %pad_add_fusion.info, bf16[4,576,256]{2,1,0:T(8,128)(2,1)S(1)} %bitcast.14, bf16[1152,128]{1,0:T(8,128)(2,1)S(1)} %get-tuple-element.46.a_ref, ...), custom_call_target="tpu_custom_call" | custom-call | tf_op jit(solution)/shard_map/spatial/pallas_call | solution.py:259
  27.1 0.1 collective-permute-start.11
  27.2 1.5 %collective-permute-done.2.ra_ref = bf16[1152,128]{1,0:T(8,128)(2,1)S(1)} collective-permute-done((bf16[1152,128]{1,0:T(8,128)(2,1)S(1)}, bf16[1152,128]{1,0:T(8,128)(2,1)S(1)}, u32[]{:S(2)}, u32[]{:S(2)}) %collective-permute-start.2) | collective-permute-done | bytes 294944 | tf_op jit(solution)/shard_map/ppermute | solution.py:252
  28.7 2.0 %collective-permute-start.15 = (bf16[64,1152]{1,0:T(8,128)(2,1)S(1)}, bf16[64,1152]{1,0:T(8,128)(2,1)S(1)}, u32[]{:S(2)}, u32[]{:S(2)}) collective-permute-start(bf16[64,1152]{1,0:T(8,128)(2,1)S(1)} %get-tuple-element.56.refs_15_), channel_id=1, source_target_pairs={{0,8},{4,12},{8,0},{12,4},{1,9},{5,13},{9,1},{13,5},{2,10},{6,14},... | collective-permute-start | bytes 442376 | tf_op jit(solution)/shard_map/ppermute | solution.py:281
  30.7 3.9 %spatial.6 = (bf16[64,1152]{1,0:T(8,128)(2,1)S(1)}, bf16[64,1152]{1,0:T(8,128)(2,1)S(1)}, bf16[64,1152]{1,0:T(8,128)(2,1)S(1)}, bf16[64,1152]{1,0:T(8,128)(2,1)S(1)}) custom-call(s32[34]{0:T(128)S(1)} %pad_add_fusion.info, bf16[4,576,256]{2,1,0:T(8,128)(2,1)S(1)} %bitcast.15, bf16[1152,128]{1,0:T(8,128)(2,1)S(1)} %get-tuple-element.43.a_ref, ...), custom_call_target="tpu_custom_call" | custom-call | tf_op jit(solution)/shard_map/spatial/pallas_call | solution.py:259
  34.6 0.1 collective-permute-start.19
  34.7 3.9 %spatial.5 = (bf16[64,1152]{1,0:T(8,128)(2,1)S(1)}, bf16[64,1152]{1,0:T(8,128)(2,1)S(1)}, bf16[64,1152]{1,0:T(8,128)(2,1)S(1)}, bf16[64,1152]{1,0:T(8,128)(2,1)S(1)}) custom-call(s32[34]{0:T(128)S(1)} %pad_add_fusion.info, bf16[4,576,256]{2,1,0:T(8,128)(2,1)S(1)} %bitcast.16, bf16[1152,128]{1,0:T(8,128)(2,1)S(1)} %get-tuple-element.40.a_ref, ...), custom_call_target="tpu_custom_call" | custom-call | tf_op jit(solution)/shard_map/spatial/pallas_call | solution.py:259
  38.7 0.2 collective-permute-start.10
  38.9 0.0 collective-permute-done.1.rb_ref
  38.9 2.0 %collective-permute-start.14 = (bf16[64,1152]{1,0:T(8,128)(2,1)S(1)}, bf16[64,1152]{1,0:T(8,128)(2,1)S(1)}, u32[]{:S(2)}, u32[]{:S(2)}) collective-permute-start(bf16[64,1152]{1,0:T(8,128)(2,1)S(1)} %get-tuple-element.55.refs_14_), channel_id=1, source_target_pairs={{0,8},{4,12},{8,0},{12,4},{1,9},{5,13},{9,1},{13,5},{2,10},{6,14},... | collective-permute-start | bytes 442376 | tf_op jit(solution)/shard_map/ppermute | solution.py:281
  40.9 0.0 collective-permute-start.18
  40.9 0.0 collective-permute-done.15.refs_11_
  40.9 0.2 collective-permute-start.9
  41.1 3.9 %spatial.4 = (bf16[64,1152]{1,0:T(8,128)(2,1)S(1)}, bf16[64,1152]{1,0:T(8,128)(2,1)S(1)}, bf16[64,1152]{1,0:T(8,128)(2,1)S(1)}, bf16[64,1152]{1,0:T(8,128)(2,1)S(1)}) custom-call(s32[34]{0:T(128)S(1)} %pad_add_fusion.info, bf16[4,576,256]{2,1,0:T(8,128)(2,1)S(1)} %bitcast.17, bf16[1152,128]{1,0:T(8,128)(2,1)S(1)} %get-tuple-element.37.a_ref, ...), custom_call_target="tpu_custom_call" | custom-call | tf_op jit(solution)/shard_map/spatial/pallas_call | solution.py:259
  45.0 0.0 collective-permute-done.19.refs_15_
  45.0 2.0 %collective-permute-start.13 = (bf16[64,1152]{1,0:T(8,128)(2,1)S(1)}, bf16[64,1152]{1,0:T(8,128)(2,1)S(1)}, u32[]{:S(2)}, u32[]{:S(2)}) collective-permute-start(bf16[64,1152]{1,0:T(8,128)(2,1)S(1)} %get-tuple-element.54.refs_13_), channel_id=1, source_target_pairs={{0,8},{4,12},{8,0},{12,4},{1,9},{5,13},{9,1},{13,5},{2,10},{6,14},... | collective-permute-start | bytes 442376 | tf_op jit(solution)/shard_map/ppermute | solution.py:281
  47.0 0.2 collective-permute-start.8
  47.2 0.4 collective-permute-done.18.refs_14_
  47.6 1.6 %collective-permute-start.12 = (bf16[64,1152]{1,0:T(8,128)(2,1)S(1)}, bf16[64,1152]{1,0:T(8,128)(2,1)S(1)}, u32[]{:S(2)}, u32[]{:S(2)}) collective-permute-start(bf16[64,1152]{1,0:T(8,128)(2,1)S(1)} %get-tuple-element.53.refs_12_), channel_id=1, source_target_pairs={{0,8},{4,12},{8,0},{12,4},{1,9},{5,13},{9,1},{13,5},{2,10},{6,14},... | collective-permute-start | bytes 442376 | tf_op jit(solution)/shard_map/ppermute | solution.py:281
  49.2 0.0 collective-permute-done.9.refs_5_
  49.2 0.3 collective-permute-start.16
  49.5 2.3 %collective-permute-done.13.refs_9_ = bf16[64,1152]{1,0:T(8,128)(2,1)S(1)} collective-permute-done((bf16[64,1152]{1,0:T(8,128)(2,1)S(1)}, bf16[64,1152]{1,0:T(8,128)(2,1)S(1)}, u32[]{:S(2)}, u32[]{:S(2)}) %collective-permute-start.13) | collective-permute-done | bytes 147488 | tf_op jit(solution)/shard_map/ppermute | solution.py:281
  51.8 2.6 %collective-permute-done.17.refs_13_ = bf16[64,1152]{1,0:T(8,128)(2,1)S(1)} collective-permute-done((bf16[64,1152]{1,0:T(8,128)(2,1)S(1)}, bf16[64,1152]{1,0:T(8,128)(2,1)S(1)}, u32[]{:S(2)}, u32[]{:S(2)}) %collective-permute-start.17) | collective-permute-done | bytes 147488 | tf_op jit(solution)/shard_map/ppermute | solution.py:281
  54.4 0.0 collective-permute-done.8.refs_4_
  54.4 3.7 %collective-permute-done.12.refs_8_ = bf16[64,1152]{1,0:T(8,128)(2,1)S(1)} collective-permute-done((bf16[64,1152]{1,0:T(8,128)(2,1)S(1)}, bf16[64,1152]{1,0:T(8,128)(2,1)S(1)}, u32[]{:S(2)}, u32[]{:S(2)}) %collective-permute-start.12) | collective-permute-done | bytes 147488 | tf_op jit(solution)/shard_map/ppermute | solution.py:281
  58.1 2.2 %collective-permute-done.16.refs_12_ = bf16[64,1152]{1,0:T(8,128)(2,1)S(1)} collective-permute-done((bf16[64,1152]{1,0:T(8,128)(2,1)S(1)}, bf16[64,1152]{1,0:T(8,128)(2,1)S(1)}, u32[]{:S(2)}, u32[]{:S(2)}) %collective-permute-start.16) | collective-permute-done | bytes 147488 | tf_op jit(solution)/shard_map/ppermute | solution.py:281
  60.3 10.4 %temporal.3 = (bf16[576,128]{1,0:T(8,128)(2,1)S(1)}, bf16[576,128]{1,0:T(8,128)(2,1)S(1)}, bf16[576,128]{1,0:T(8,128)(2,1)S(1)}, bf16[576,128]{1,0:T(8,128)(2,1)S(1)}) custom-call(bf16[64,1152]{1,0:T(8,128)(2,1)S(1)} %get-tuple-element.39.refs_0_.refs_4_, bf16[64,1152]{1,0:T(8,128)(2,1)S(1)} %get-tuple-element.42.refs_1_.refs_5_, ...), custom_call_target="tpu_custom_call" | custom-call | tf_op jit(solution)/shard_map/temporal/pallas_call | solution.py:292
  70.8 0.4 collective-permute-start.23
  71.1 1.7 %collective-permute-start.24 = (bf16[576,128]{1,0:T(8,128)(2,1)S(1)}, bf16[576,128]{1,0:T(8,128)(2,1)S(1)}, u32[]{:S(2)}, u32[]{:S(2)}) collective-permute-start(bf16[576,128]{1,0:T(8,128)(2,1)S(1)} %get-tuple-element.67), channel_id=1, source_target_pairs={{8,0},{12,4},{0,8},{4,12},{9,1},{13,5},{1,9},{5,13},{10,2},{14,6},... | collective-permute-start | bytes 442376 | tf_op jit(solution)/shard_map/ppermute | solution.py:309
  72.8 0.0 collective-permute-start.25
  72.8 10.4 %temporal.2 = (bf16[576,128]{1,0:T(8,128)(2,1)S(1)}, bf16[576,128]{1,0:T(8,128)(2,1)S(1)}, bf16[576,128]{1,0:T(8,128)(2,1)S(1)}, bf16[576,128]{1,0:T(8,128)(2,1)S(1)}) custom-call(bf16[64,1152]{1,0:T(8,128)(2,1)S(1)} %get-tuple-element.39.refs_0_.refs_4_, bf16[64,1152]{1,0:T(8,128)(2,1)S(1)} %get-tuple-element.42.refs_1_.refs_5_, ...), custom_call_target="tpu_custom_call" | custom-call | tf_op jit(solution)/shard_map/temporal/pallas_call | solution.py:292
  83.2 0.4 collective-permute-start.20
  83.6 1.7 %collective-permute-start.21 = (bf16[576,128]{1,0:T(8,128)(2,1)S(1)}, bf16[576,128]{1,0:T(8,128)(2,1)S(1)}, u32[]{:S(2)}, u32[]{:S(2)}) collective-permute-start(bf16[576,128]{1,0:T(8,128)(2,1)S(1)} %get-tuple-element.63), channel_id=1, source_target_pairs={{8,0},{12,4},{0,8},{4,12},{9,1},{13,5},{1,9},{5,13},{10,2},{14,6},... | collective-permute-start | bytes 442376 | tf_op jit(solution)/shard_map/ppermute | solution.py:309
  85.3 0.0 collective-permute-done.25.refs_3_
  85.3 2.8 %output.2.refs_22_ = bf16[4,256,1152]{2,1,0:T(8,128)(2,1)} custom-call(s32[34]{0:T(128)S(1)} %pad_add_fusion.info, bf16[576,128]{1,0:T(8,128)(2,1)S(1)} %get-tuple-element.65.refs_0_, bf16[576,128]{1,0:T(8,128)(2,1)S(1)} %collective-permute-done.23.refs_1_, bf16[576,128]{1,0:T(8,128)(2,1)S(1)} %collective-permute-done.24.refs_2_, ...), custom_call_target="tpu_custom_call" | custom-call | tf_op jit(solution)/shard_map/output/pallas_call | solution.py:315
  88.2 2.2 %collective-permute-done.21.refs_2_ = bf16[576,128]{1,0:T(8,128)(2,1)S(1)} collective-permute-done((bf16[576,128]{1,0:T(8,128)(2,1)S(1)}, bf16[576,128]{1,0:T(8,128)(2,1)S(1)}, u32[]{:S(2)}, u32[]{:S(2)}) %collective-permute-start.21) | collective-permute-done | bytes 147488 | tf_op jit(solution)/shard_map/ppermute | solution.py:309
  90.3 1.6 %collective-permute-done.22.refs_3_ = bf16[576,128]{1,0:T(8,128)(2,1)S(1)} collective-permute-done((bf16[576,128]{1,0:T(8,128)(2,1)S(1)}, bf16[576,128]{1,0:T(8,128)(2,1)S(1)}, u32[]{:S(2)}, u32[]{:S(2)}) %collective-permute-start.22) | collective-permute-done | bytes 147488 | tf_op jit(solution)/shard_map/ppermute | solution.py:309
  91.9 2.8 %output.3 = bf16[4,256,1152]{2,1,0:T(8,128)(2,1)} custom-call(s32[34]{0:T(128)S(1)} %pad_add_fusion.info, bf16[576,128]{1,0:T(8,128)(2,1)S(1)} %get-tuple-element.61.refs_0_, bf16[576,128]{1,0:T(8,128)(2,1)S(1)} %collective-permute-done.20.refs_1_, bf16[576,128]{1,0:T(8,128)(2,1)S(1)} %collective-permute-done.21.refs_2_, ...), custom_call_target="tpu_custom_call", output_to_operand_aliasing={{}: (23, {})} | custom-call | tf_op jit(solution)/shard_map/output/pallas_call | solution.py:315
  (23 shorter events, 0.1 us)
Async XLA Ops:
  1.8 1.3 %copy-start.2 = (bf16[4,256,576]{1,2,0:T(8,128)(2,1)S(1)}, bf16[4,256,576]{1,2,0:T(8,128)(2,1)}, u32[]{:S(2)}) copy-start(bf16[4,256,576]{1,2,0:T(8,128)(2,1)} %param.12) | copy-start | bytes 3538948
  3.1 1.3 %copy-start.3 = (bf16[4,256,576]{1,2,0:T(8,128)(2,1)S(1)}, bf16[4,256,576]{1,2,0:T(8,128)(2,1)}, u32[]{:S(2)}) copy-start(bf16[4,256,576]{1,2,0:T(8,128)(2,1)} %param.13) | copy-start | bytes 3538948
  5.1 11.8 %collective-permute-start.6 = (bf16[1152,128]{1,0:T(8,128)(2,1)S(1)}, bf16[1152,128]{1,0:T(8,128)(2,1)S(1)}, u32[]{:S(2)}, u32[]{:S(2)}) collective-permute-start(bf16[1152,128]{1,0:T(8,128)(2,1)S(1)} %get-tuple-element.46.a_ref), channel_id=1, source_target_pairs={{0,1},{1,0},{2,3},{3,2},{4,5},{5,4},{6,7},{7,6},{8,9},{9,8},{10,11... | collective-permute-start | bytes 884744 | tf_op jit(solution)/shard_map/ppermute | solution.py:252
  8.2 10.1 %collective-permute-start.7 = (bf16[1152,128]{1,0:T(8,128)(2,1)S(1)}, bf16[1152,128]{1,0:T(8,128)(2,1)S(1)}, u32[]{:S(2)}, u32[]{:S(2)}) collective-permute-start(bf16[1152,128]{1,0:T(8,128)(2,1)S(1)} %get-tuple-element.47.b_ref), channel_id=1, source_target_pairs={{1,2},{2,1},{5,6},{6,5},{9,10},{10,9},{13,14},{14,13},{17,18},{18,... | collective-permute-start | bytes 884744 | tf_op jit(solution)/shard_map/ppermute | solution.py:252
  8.9 14.2 %copy-start.4 = (bf16[4,256,576]{1,2,0:T(8,128)(2,1)S(1)}, bf16[4,256,576]{1,2,0:T(8,128)(2,1)}, u32[]{:S(2)}) copy-start(bf16[4,256,576]{1,2,0:T(8,128)(2,1)} %param.11) | copy-start | bytes 3538948
  9.6 12.8 %collective-permute-start.4 = (bf16[1152,128]{1,0:T(8,128)(2,1)S(1)}, bf16[1152,128]{1,0:T(8,128)(2,1)S(1)}, u32[]{:S(2)}, u32[]{:S(2)}) collective-permute-start(bf16[1152,128]{1,0:T(8,128)(2,1)S(1)} %get-tuple-element.43.a_ref), channel_id=1, source_target_pairs={{0,1},{1,0},{2,3},{3,2},{4,5},{5,4},{6,7},{7,6},{8,9},{9,8},{10,11... | collective-permute-start | bytes 884744 | tf_op jit(solution)/shard_map/ppermute | solution.py:252
  14.1 13.0 %collective-permute-start.5 = (bf16[1152,128]{1,0:T(8,128)(2,1)S(1)}, bf16[1152,128]{1,0:T(8,128)(2,1)S(1)}, u32[]{:S(2)}, u32[]{:S(2)}) collective-permute-start(bf16[1152,128]{1,0:T(8,128)(2,1)S(1)} %get-tuple-element.44.b_ref), channel_id=1, source_target_pairs={{1,2},{2,1},{5,6},{6,5},{9,10},{10,9},{13,14},{14,13},{17,18},{18,... | collective-permute-start | bytes 884744 | tf_op jit(solution)/shard_map/ppermute | solution.py:252
  14.8 8.3 %copy-start.1 = (bf16[576,1152]{1,0:T(8,128)(2,1)S(1)}, bf16[576,1152]{1,0:T(8,128)(2,1)}, u32[]{:S(2)}) copy-start(bf16[576,1152]{1,0:T(8,128)(2,1)} %w_ref.7) | copy-start | bytes 3981316
  15.5 7.6 %copy-start.6 = (f32[1152]{0:T(1024)S(1)}, f32[1152]{0:T(1024)}, u32[]{:S(2)}) copy-start(f32[1152]{0:T(1024)} %param.16) | copy-start | bytes 13828
  15.5 7.6 %copy-start = (bf16[4,256,1152]{2,1,0:T(8,128)(2,1)S(1)}, bf16[4,256,1152]{2,1,0:T(8,128)(2,1)}, u32[]{:S(2)}) copy-start(bf16[4,256,1152]{2,1,0:T(8,128)(2,1)} %h_ref.7) | copy-start | bytes 7077892
  15.5 13.2 %collective-permute-start.2 = (bf16[1152,128]{1,0:T(8,128)(2,1)S(1)}, bf16[1152,128]{1,0:T(8,128)(2,1)S(1)}, u32[]{:S(2)}, u32[]{:S(2)}) collective-permute-start(bf16[1152,128]{1,0:T(8,128)(2,1)S(1)} %get-tuple-element.40.a_ref), channel_id=1, source_target_pairs={{0,1},{1,0},{2,3},{3,2},{4,5},{5,4},{6,7},{7,6},{8,9},{9,8},{10,11... | collective-permute-start | bytes 884744 | tf_op jit(solution)/shard_map/ppermute | solution.py:252
  16.9 17.7 %collective-permute-start.3 = (bf16[1152,128]{1,0:T(8,128)(2,1)S(1)}, bf16[1152,128]{1,0:T(8,128)(2,1)S(1)}, u32[]{:S(2)}, u32[]{:S(2)}) collective-permute-start(bf16[1152,128]{1,0:T(8,128)(2,1)S(1)} %get-tuple-element.41.b_ref), channel_id=1, source_target_pairs={{1,2},{2,1},{5,6},{6,5},{9,10},{10,9},{13,14},{14,13},{17,18},{18,... | collective-permute-start | bytes 884744 | tf_op jit(solution)/shard_map/ppermute | solution.py:252
  18.3 20.4 %collective-permute-start = (bf16[1152,128]{1,0:T(8,128)(2,1)S(1)}, bf16[1152,128]{1,0:T(8,128)(2,1)S(1)}, u32[]{:S(2)}, u32[]{:S(2)}) collective-permute-start(bf16[1152,128]{1,0:T(8,128)(2,1)S(1)} %get-tuple-element.37.a_ref), channel_id=1, source_target_pairs={{0,1},{1,0},{2,3},{3,2},{4,5},{5,4},{6,7},{7,6},{8,9},{9,8},{10,11... | collective-permute-start | bytes 884744 | tf_op jit(solution)/shard_map/ppermute | solution.py:252
  22.4 16.5 %collective-permute-start.1 = (bf16[1152,128]{1,0:T(8,128)(2,1)S(1)}, bf16[1152,128]{1,0:T(8,128)(2,1)S(1)}, u32[]{:S(2)}, u32[]{:S(2)}) collective-permute-start(bf16[1152,128]{1,0:T(8,128)(2,1)S(1)} %get-tuple-element.38.b_ref), channel_id=1, source_target_pairs={{1,2},{2,1},{5,6},{6,5},{9,10},{10,9},{13,14},{14,13},{17,18},{18,... | collective-permute-start | bytes 884744 | tf_op jit(solution)/shard_map/ppermute | solution.py:252
  27.1 13.8 %collective-permute-start.11 = (bf16[64,1152]{1,0:T(8,128)(2,1)S(1)}, bf16[64,1152]{1,0:T(8,128)(2,1)S(1)}, u32[]{:S(2)}, u32[]{:S(2)}) collective-permute-start(bf16[64,1152]{1,0:T(8,128)(2,1)S(1)} %get-tuple-element.52.refs_11_), channel_id=1, source_target_pairs={{0,4},{4,0},{8,12},{12,8},{1,5},{5,1},{9,13},{13,9},{2,6},{6,2},{1... | collective-permute-start | bytes 442376 | tf_op jit(solution)/shard_map/ppermute | solution.py:281
  28.7 12.2 %collective-permute-start.15 = (bf16[64,1152]{1,0:T(8,128)(2,1)S(1)}, bf16[64,1152]{1,0:T(8,128)(2,1)S(1)}, u32[]{:S(2)}, u32[]{:S(2)}) collective-permute-start(bf16[64,1152]{1,0:T(8,128)(2,1)S(1)} %get-tuple-element.56.refs_15_), channel_id=1, source_target_pairs={{0,8},{4,12},{8,0},{12,4},{1,9},{5,13},{9,1},{13,5},{2,10},{6,14},... | collective-permute-start | bytes 442376 | tf_op jit(solution)/shard_map/ppermute | solution.py:281
  34.6 10.4 %collective-permute-start.19 = (bf16[64,1152]{1,0:T(8,128)(2,1)S(1)}, bf16[64,1152]{1,0:T(8,128)(2,1)S(1)}, u32[]{:S(2)}, u32[]{:S(2)}) collective-permute-start(bf16[64,1152]{1,0:T(8,128)(2,1)S(1)} %get-tuple-element.60.refs_19_), channel_id=1, source_target_pairs={{0,12},{4,8},{8,4},{12,0},{1,13},{5,9},{9,5},{13,1},{2,14},{6,10},... | collective-permute-start | bytes 442376 | tf_op jit(solution)/shard_map/ppermute | solution.py:281
  38.7 8.4 %collective-permute-start.10 = (bf16[64,1152]{1,0:T(8,128)(2,1)S(1)}, bf16[64,1152]{1,0:T(8,128)(2,1)S(1)}, u32[]{:S(2)}, u32[]{:S(2)}) collective-permute-start(bf16[64,1152]{1,0:T(8,128)(2,1)S(1)} %get-tuple-element.51.refs_10_), channel_id=1, source_target_pairs={{0,4},{4,0},{8,12},{12,8},{1,5},{5,1},{9,13},{13,9},{2,6},{6,2},{1... | collective-permute-start | bytes 442376 | tf_op jit(solution)/shard_map/ppermute | solution.py:281
  38.9 8.1 %collective-permute-start.14 = (bf16[64,1152]{1,0:T(8,128)(2,1)S(1)}, bf16[64,1152]{1,0:T(8,128)(2,1)S(1)}, u32[]{:S(2)}, u32[]{:S(2)}) collective-permute-start(bf16[64,1152]{1,0:T(8,128)(2,1)S(1)} %get-tuple-element.55.refs_14_), channel_id=1, source_target_pairs={{0,8},{4,12},{8,0},{12,4},{1,9},{5,13},{9,1},{13,5},{2,10},{6,14},... | collective-permute-start | bytes 442376 | tf_op jit(solution)/shard_map/ppermute | solution.py:281
  40.9 6.7 %collective-permute-start.18 = (bf16[64,1152]{1,0:T(8,128)(2,1)S(1)}, bf16[64,1152]{1,0:T(8,128)(2,1)S(1)}, u32[]{:S(2)}, u32[]{:S(2)}) collective-permute-start(bf16[64,1152]{1,0:T(8,128)(2,1)S(1)} %get-tuple-element.59.refs_18_), channel_id=1, source_target_pairs={{0,12},{4,8},{8,4},{12,0},{1,13},{5,9},{9,5},{13,1},{2,14},{6,10},... | collective-permute-start | bytes 442376 | tf_op jit(solution)/shard_map/ppermute | solution.py:281
  40.9 8.3 %collective-permute-start.9 = (bf16[64,1152]{1,0:T(8,128)(2,1)S(1)}, bf16[64,1152]{1,0:T(8,128)(2,1)S(1)}, u32[]{:S(2)}, u32[]{:S(2)}) collective-permute-start(bf16[64,1152]{1,0:T(8,128)(2,1)S(1)} %get-tuple-element.50.refs_9_), channel_id=1, source_target_pairs={{0,4},{4,0},{8,12},{12,8},{1,5},{5,1},{9,13},{13,9},{2,6},{6,2},{1... | collective-permute-start | bytes 442376 | tf_op jit(solution)/shard_map/ppermute | solution.py:281
  45.0 6.8 %collective-permute-start.13 = (bf16[64,1152]{1,0:T(8,128)(2,1)S(1)}, bf16[64,1152]{1,0:T(8,128)(2,1)S(1)}, u32[]{:S(2)}, u32[]{:S(2)}) collective-permute-start(bf16[64,1152]{1,0:T(8,128)(2,1)S(1)} %get-tuple-element.54.refs_13_), channel_id=1, source_target_pairs={{0,8},{4,12},{8,0},{12,4},{1,9},{5,13},{9,1},{13,5},{2,10},{6,14},... | collective-permute-start | bytes 442376 | tf_op jit(solution)/shard_map/ppermute | solution.py:281
  47.0 7.4 %collective-permute-start.17 = (bf16[64,1152]{1,0:T(8,128)(2,1)S(1)}, bf16[64,1152]{1,0:T(8,128)(2,1)S(1)}, u32[]{:S(2)}, u32[]{:S(2)}) collective-permute-start(bf16[64,1152]{1,0:T(8,128)(2,1)S(1)} %get-tuple-element.58.refs_17_), channel_id=1, source_target_pairs={{0,12},{4,8},{8,4},{12,0},{1,13},{5,9},{9,5},{13,1},{2,14},{6,10},... | collective-permute-start | bytes 442376 | tf_op jit(solution)/shard_map/ppermute | solution.py:281
  47.0 7.4 %collective-permute-start.8 = (bf16[64,1152]{1,0:T(8,128)(2,1)S(1)}, bf16[64,1152]{1,0:T(8,128)(2,1)S(1)}, u32[]{:S(2)}, u32[]{:S(2)}) collective-permute-start(bf16[64,1152]{1,0:T(8,128)(2,1)S(1)} %get-tuple-element.49.refs_8_), channel_id=1, source_target_pairs={{0,4},{4,0},{8,12},{12,8},{1,5},{5,1},{9,13},{13,9},{2,6},{6,2},{1... | collective-permute-start | bytes 442376 | tf_op jit(solution)/shard_map/ppermute | solution.py:281
  47.6 10.5 %collective-permute-start.12 = (bf16[64,1152]{1,0:T(8,128)(2,1)S(1)}, bf16[64,1152]{1,0:T(8,128)(2,1)S(1)}, u32[]{:S(2)}, u32[]{:S(2)}) collective-permute-start(bf16[64,1152]{1,0:T(8,128)(2,1)S(1)} %get-tuple-element.53.refs_12_), channel_id=1, source_target_pairs={{0,8},{4,12},{8,0},{12,4},{1,9},{5,13},{9,1},{13,5},{2,10},{6,14},... | collective-permute-start | bytes 442376 | tf_op jit(solution)/shard_map/ppermute | solution.py:281
  49.2 11.1 %collective-permute-start.16 = (bf16[64,1152]{1,0:T(8,128)(2,1)S(1)}, bf16[64,1152]{1,0:T(8,128)(2,1)S(1)}, u32[]{:S(2)}, u32[]{:S(2)}) collective-permute-start(bf16[64,1152]{1,0:T(8,128)(2,1)S(1)} %get-tuple-element.57.refs_16_), channel_id=1, source_target_pairs={{0,12},{4,8},{8,4},{12,0},{1,13},{5,9},{9,5},{13,1},{2,14},{6,10},... | collective-permute-start | bytes 442376 | tf_op jit(solution)/shard_map/ppermute | solution.py:281
  70.8 14.5 %collective-permute-start.23 = (bf16[576,128]{1,0:T(8,128)(2,1)S(1)}, bf16[576,128]{1,0:T(8,128)(2,1)S(1)}, u32[]{:S(2)}, u32[]{:S(2)}) collective-permute-start(bf16[576,128]{1,0:T(8,128)(2,1)S(1)} %get-tuple-element.66), channel_id=1, source_target_pairs={{4,0},{0,4},{12,8},{8,12},{5,1},{1,5},{13,9},{9,13},{6,2},{2,6},{1... | collective-permute-start | bytes 442376 | tf_op jit(solution)/shard_map/ppermute | solution.py:309
  71.1 14.2 %collective-permute-start.24 = (bf16[576,128]{1,0:T(8,128)(2,1)S(1)}, bf16[576,128]{1,0:T(8,128)(2,1)S(1)}, u32[]{:S(2)}, u32[]{:S(2)}) collective-permute-start(bf16[576,128]{1,0:T(8,128)(2,1)S(1)} %get-tuple-element.67), channel_id=1, source_target_pairs={{8,0},{12,4},{0,8},{4,12},{9,1},{13,5},{1,9},{5,13},{10,2},{14,6},... | collective-permute-start | bytes 442376 | tf_op jit(solution)/shard_map/ppermute | solution.py:309
  72.8 12.5 %copy-start.7 = (f32[1152]{0:T(1024)S(1)}, f32[1152]{0:T(1024)}, u32[]{:S(2)}) copy-start(f32[1152]{0:T(1024)} %param.19) | copy-start | bytes 13828
  72.8 12.5 %copy-start.5 = (bf16[576,1152]{1,0:T(8,128)(2,1)S(1)}, bf16[576,1152]{1,0:T(8,128)(2,1)}, u32[]{:S(2)}) copy-start(bf16[576,1152]{1,0:T(8,128)(2,1)} %refs_20_.3) | copy-start | bytes 3981316
  72.8 12.5 %collective-permute-start.25 = (bf16[576,128]{1,0:T(8,128)(2,1)S(1)}, bf16[576,128]{1,0:T(8,128)(2,1)S(1)}, u32[]{:S(2)}, u32[]{:S(2)}) collective-permute-start(bf16[576,128]{1,0:T(8,128)(2,1)S(1)} %get-tuple-element.68), channel_id=1, source_target_pairs={{12,0},{8,4},{4,8},{0,12},{13,1},{9,5},{5,9},{1,13},{14,2},{10,6},... | collective-permute-start | bytes 442376 | tf_op jit(solution)/shard_map/ppermute | solution.py:309
  83.2 5.0 %collective-permute-start.20 = (bf16[576,128]{1,0:T(8,128)(2,1)S(1)}, bf16[576,128]{1,0:T(8,128)(2,1)S(1)}, u32[]{:S(2)}, u32[]{:S(2)}) collective-permute-start(bf16[576,128]{1,0:T(8,128)(2,1)S(1)} %get-tuple-element.62), channel_id=1, source_target_pairs={{4,0},{0,4},{12,8},{8,12},{5,1},{1,5},{13,9},{9,13},{6,2},{2,6},{1... | collective-permute-start | bytes 442376 | tf_op jit(solution)/shard_map/ppermute | solution.py:309
  83.6 6.7 %collective-permute-start.21 = (bf16[576,128]{1,0:T(8,128)(2,1)S(1)}, bf16[576,128]{1,0:T(8,128)(2,1)S(1)}, u32[]{:S(2)}, u32[]{:S(2)}) collective-permute-start(bf16[576,128]{1,0:T(8,128)(2,1)S(1)} %get-tuple-element.63), channel_id=1, source_target_pairs={{8,0},{12,4},{0,8},{4,12},{9,1},{13,5},{1,9},{5,13},{10,2},{14,6},... | collective-permute-start | bytes 442376 | tf_op jit(solution)/shard_map/ppermute | solution.py:309
  85.3 6.6 %collective-permute-start.22 = (bf16[576,128]{1,0:T(8,128)(2,1)S(1)}, bf16[576,128]{1,0:T(8,128)(2,1)S(1)}, u32[]{:S(2)}, u32[]{:S(2)}) collective-permute-start(bf16[576,128]{1,0:T(8,128)(2,1)S(1)} %get-tuple-element.64), channel_id=1, source_target_pairs={{12,0},{8,4},{4,8},{0,12},{13,1},{9,5},{5,9},{1,13},{14,2},{10,6},... | collective-permute-start | bytes 442376 | tf_op jit(solution)/shard_map/ppermute | solution.py:309
